TPU v7x, 32 devices: a whole 2x2x4 slice. The times are simulated.
32 devices in a mesh: leaf: 4 (over z), row: 2 (over x), top: 4 (over y, core).
Axes of the slice: x: 2, y: 2, z: 4, core: 2. Of those that a mesh axis runs over, the one named last changes fastest.
Arguments:
- loads: bfloat16 [4, 2, 4, 1, 256, 32], P('leaf', 'row', 'top'), may hold values from -6 to 6
- flux_maps: bfloat16 [4, 2, 4, 640, 256], P('leaf', 'row', 'top'), may hold values from -0.375 to 0.375
- chain_maps: float32 [4, 2, 4, 640, 640], P('leaf', 'row', 'top')
- leaf_maps: bfloat16 [4, 2, 4, 1, 256, 256], P('leaf', 'row', 'top'), may hold values from -0.375 to 0.375
- edge_maps: bfloat16 [4, 2, 4, 1, 256, 640], P('leaf', 'row', 'top'), may hold values from -0.25 to 0.25
- top_maps: bfloat16 [4, 2, 4, 1, 256, 128], P('leaf', 'row', 'top'), may hold values from -0.5 to 0.5
- slot_nodes: int32 [4, 2, 4, 128], P('leaf', 'row', 'top'), may hold values from 0 to 8191
- slot_counts: int32 [4, 2, 4], P('leaf', 'row', 'top'), may hold values from 1 to 128, 320 in all within a row
- top_loads: float32 [8192, 32], P('leaf'), may hold values from -6 to 6
- top_inverse: float32 [8192, 8192], P('top', ('leaf', 'row')), may hold values from -0.0625 to 0.0625
Outputs:
- solution: bfloat16 [4, 2, 4, 1, 256, 32], P('leaf', 'row', 'top')
- top_values: float32 [8192, 32], P('top')
Inputs may be any that keep to these rules, and one draw needn't show every extreme that they name: `slot_counts`: over the 4 subtrees of one x-y cell (same x and y, all t) the live slots sum to 320, and one of those subtrees has all 128 slots live.
All inputs are finite; a program needn't handle non-finite values. No bound on the sum of `slot_counts` on one device may be relied on, other than what follows from the above.
Results may differ from a plain program's by a relative error of at most 0.0046.
Values sent between devices are 32-bit elements; how exact they have to be, the bound alone decides.
A program may use at most 64 MiB of HBM per device.

v0:
```python
import jax
import jax.numpy as jnp
from jax import lax
from jax.sharding import PartitionSpec as P


def passed_along(value, axis, steps):
    count = lax.axis_size(axis)
    first, last = (max(0, -steps), min(count, count - steps))
    return lax.ppermute(value, axis, [(source, source + steps) for source in range(first, last)])


def body(
    loads,
    flux_maps,
    chain_maps,
    leaf_maps,
    edge_maps,
    top_maps,
    slot_nodes,
    slot_counts,
    top_loads,
    top_inverse,
):
    leaf_count = loads.shape[3]
    node_count = loads.shape[4]
    rhs_count = loads.shape[5]
    sep_width = chain_maps.shape[-1]
    slot_total = slot_nodes.shape[-1]
    largest_level = lax.Precision.HIGHEST
    local_loads = loads.reshape(leaf_count, node_count, rhs_count)
    flattened = loads.reshape(leaf_count * node_count, rhs_count)
    fluxes = jnp.dot(
        flux_maps.reshape(sep_width, leaf_count * node_count),
        flattened,
        preferred_element_type=jnp.float32,
    )
    combine_operator = chain_maps.reshape(sep_width, sep_width)
    chain_index = lax.axis_index("leaf")

    def advance(step_index, carried):
        earlier = passed_along(carried, "leaf", 1)
        advanced = (
            jnp.dot(
                combine_operator,
                earlier,
                precision=largest_level,
                preferred_element_type=jnp.float32,
            )
            + fluxes
        )
        return jnp.where(chain_index == step_index, advanced, carried)

    states = lax.fori_loop(1, lax.axis_size("leaf"), advance, fluxes)
    slot_ids = slot_nodes.reshape(slot_total)
    is_live = lax.iota(jnp.int32, slot_total) < slot_counts.reshape(())
    chosen_entries = jnp.where(is_live[:, None], states[:slot_total], jnp.float32(0.0))
    block_rows = top_loads.shape[0]
    row_ids = lax.iota(jnp.int32, block_rows * lax.axis_size("leaf"))
    match_table = (row_ids[:, None] == slot_ids[None, :]).astype(jnp.float32)
    top_block = lax.psum_scatter(
        jnp.dot(
            match_table, chosen_entries, precision=largest_level, preferred_element_type=jnp.float32
        ),
        "leaf",
        scatter_dimension=0,
        tiled=True,
    )
    top_block = lax.psum(top_block, ("row", "top"))
    rhs_block = top_loads - top_block
    column_rows = top_inverse.shape[1]
    rhs_piece = lax.dynamic_slice_in_dim(
        rhs_block, lax.axis_index("row") * column_rows, column_rows, 0
    )
    partial_value = jnp.dot(
        top_inverse, rhs_piece, precision=largest_level, preferred_element_type=jnp.float32
    )
    owned_rows = lax.psum(partial_value, ("leaf", "row"))
    shard_piece = lax.all_gather(owned_rows, "top", axis=0, tiled=True)
    row_ids = lax.iota(jnp.int32, shard_piece.shape[0])
    match_table = ((slot_ids[:, None] == row_ids[None, :]) & is_live[:, None]).astype(jnp.float32)
    boundary = jnp.dot(
        match_table, shard_piece, precision=largest_level, preferred_element_type=jnp.float32
    )
    states_low = states.astype(jnp.bfloat16)
    boundary_low = boundary.astype(jnp.bfloat16)
    summed = jnp.einsum(
        "lij,ljr->lir",
        leaf_maps.reshape(leaf_count, node_count, node_count),
        local_loads,
        preferred_element_type=jnp.float32,
    )
    summed = summed + jnp.einsum(
        "lik,kr->lir",
        edge_maps.reshape(leaf_count, node_count, sep_width),
        states_low,
        preferred_element_type=jnp.float32,
    )
    summed = summed + jnp.einsum(
        "lic,cr->lir",
        top_maps.reshape(leaf_count, node_count, slot_total),
        boundary_low,
        preferred_element_type=jnp.float32,
    )
    solution = summed.astype(jnp.bfloat16).reshape(1, 1, 1, leaf_count, node_count, rhs_count)
    return (solution, owned_rows)


def solution(mesh):
    in_specs = (
        P("leaf", "row", "top", None, None, None),
        P("leaf", "row", "top", None, None),
        P("leaf", "row", "top", None, None),
        P("leaf", "row", "top", None, None, None),
        P("leaf", "row", "top", None, None, None),
        P("leaf", "row", "top", None, None, None),
        P("leaf", "row", "top", None),
        P("leaf", "row", "top"),
        P("leaf", None),
        P("top", ("leaf", "row")),
    )
    out_specs = (P("leaf", "row", "top", None, None, None), P("top", None))
    return jax.shard_map(body, mesh=mesh, in_specs=in_specs, out_specs=out_specs, check_vma=False)
```

profile of v0, /device:TPU:0, one launch (start us, length us, event | category | flops | bytes accessed | tf_op | source)
XLA Modules:
  0.0 237.6 jit_solution(16142841711911786712)
XLA Ops:
  7.9 0.2 copy-done
  8.2 0.9 fusion.15
  9.1 29.0 %while.13 = (s32[]{:T(128)}, f32[640,32]{0,1:T(8,128)S(1)}, s32[]{:T(128)}, f32[640,640]{1,0:T(8,128)}, f32[640,32]{0,1:T(8,128)S(1)}, /*index=5*/s32[]{:T(128)}) while((s32[]{:T(128)}, f32[640,32]{0,1:T(8,128)S(1)}, s32[]{:T(128)}, f32[640,640]{1,0:T(8,128)}, f32[640,32]{0,1:T(8,128)S(1)}, /*index=5*/s32[]{:T(128)}) %tuple.44), condition=%wide.region_1.2_spmd, body=%wide.region_0.1_spmd.sunk | while | flops 157327360 | bytes 2293879 | solution.py:54
  9.1 5.1 %collective-permute-start = (f32[640,32]{0,1:T(8,128)S(1)}, f32[640,32]{0,1:T(8,128)S(1)}, u32[]{:S(2)}, u32[]{:S(2)}) collective-permute-start(f32[640,32]{0,1:T(8,128)S(1)} %get-tuple-element.145), channel_id=1, source_target_pairs={{0,8},{8,16},{16,24},{1,9},{9,17},{17,25},{2,10},{10,18},{18,26},{... | collective-permute-start | bytes 245768 | tf_op jit(solution)/shard_map/while/body/eval_jaxpr/ppermute | solution.py:10
  14.2 2.0 collective-permute-done
  16.3 3.1 %fusion.39 = f32[640,32]{0,1:T(8,128)S(1)} fusion(f32[640,32]{0,1:T(8,128)S(1)} %get-tuple-element.145, f32[640,32]{0,1:T(8,128)S(1)} %get-tuple-element.154, f32[640,640]{1,0:T(8,128)} %get-tuple-element.153, f32[640,32]{0,1:T(8,128)S(1)} %collective-permute-done, pred[]{:T(512)S(6)} %eq.69), kind=kOutput, calls=%fused_computation.1.clone.1 | convolution fusion | flops 157327360 | bytes 1966081 | tf_op jit(solution)/shard_map/while/body/eval_jaxpr/dot_general | solution.py:44
  19.4 4.3 %collective-permute-start = (f32[640,32]{0,1:T(8,128)S(1)}, f32[640,32]{0,1:T(8,128)S(1)}, u32[]{:S(2)}, u32[]{:S(2)}) collective-permute-start(f32[640,32]{0,1:T(8,128)S(1)} %get-tuple-element.145), channel_id=1, source_target_pairs={{0,8},{8,16},{16,24},{1,9},{9,17},{17,25},{2,10},{10,18},{18,26},{... | collective-permute-start | bytes 245768 | tf_op jit(solution)/shard_map/while/body/eval_jaxpr/ppermute | solution.py:10
  23.7 2.0 collective-permute-done
  25.7 3.1 %fusion.39 = f32[640,32]{0,1:T(8,128)S(1)} fusion(f32[640,32]{0,1:T(8,128)S(1)} %get-tuple-element.145, f32[640,32]{0,1:T(8,128)S(1)} %get-tuple-element.154, f32[640,640]{1,0:T(8,128)} %get-tuple-element.153, f32[640,32]{0,1:T(8,128)S(1)} %collective-permute-done, pred[]{:T(512)S(6)} %eq.69), kind=kOutput, calls=%fused_computation.1.clone.1 | convolution fusion | flops 157327360 | bytes 1966081 | tf_op jit(solution)/shard_map/while/body/eval_jaxpr/dot_general | solution.py:44
  28.8 4.3 %collective-permute-start = (f32[640,32]{0,1:T(8,128)S(1)}, f32[640,32]{0,1:T(8,128)S(1)}, u32[]{:S(2)}, u32[]{:S(2)}) collective-permute-start(f32[640,32]{0,1:T(8,128)S(1)} %get-tuple-element.145), channel_id=1, source_target_pairs={{0,8},{8,16},{16,24},{1,9},{9,17},{17,25},{2,10},{10,18},{18,26},{... | collective-permute-start | bytes 245768 | tf_op jit(solution)/shard_map/while/body/eval_jaxpr/ppermute | solution.py:10
  33.1 2.0 collective-permute-done
  35.1 3.1 %fusion.39 = f32[640,32]{0,1:T(8,128)S(1)} fusion(f32[640,32]{0,1:T(8,128)S(1)} %get-tuple-element.145, f32[640,32]{0,1:T(8,128)S(1)} %get-tuple-element.154, f32[640,640]{1,0:T(8,128)} %get-tuple-element.153, f32[640,32]{0,1:T(8,128)S(1)} %collective-permute-done, pred[]{:T(512)S(6)} %eq.69), kind=kOutput, calls=%fused_computation.1.clone.1 | convolution fusion | flops 157327360 | bytes 1966081 | tf_op jit(solution)/shard_map/while/body/eval_jaxpr/dot_general | solution.py:44
  38.2 3.3 %fusion.2 = f32[8192,32]{0,1:T(8,128)} fusion(s32[128]{0:T(128)S(1)} %bitcast.45, f32[640,32]{0,1:T(8,128)S(1)} %get-tuple-element.96, pred[128]{0:T(512)(128)(4,1)S(1)} %iota_compare_fusion.3), kind=kOutput, calls=%fused_computation.5 | convolution fusion | flops 403705856 | bytes 1065984 | tf_op jit(solution)/shard_map/dot_general | solution.py:62
  41.6 29.4 %reduce-scatter.2.cloned.1.call-done = f32[2048,32]{0,1:T(8,128)} async-done(((f32[8192,32]{0,1:T(8,128)}), f32[2048,32]{0,1:T(8,128)}) %reduce-scatter.2.cloned.1.call-update) | async-done | bytes 262160 | tf_op jit(solution)/shard_map/reduce_scatter | solution.py:61
  71.1 55.4 %all-reduce.3.cloned.1.call-done = f32[2048,32]{0,1:T(8,128)} async-done(((f32[2048,32]{0,1:T(8,128)}), f32[2048,32]{0,1:T(8,128)}) %all-reduce.3.cloned.1.call-update) | async-done | bytes 262160 | tf_op jit(solution)/shard_map/psum | solution.py:69
  126.5 11.7 %convolution_bitcast_fusion = f32[2048,32]{0,1:T(8,128)} fusion(f32[2048,1024]{1,0:T(8,128)} %param.21, f32[2048,32]{0,1:T(8,128)} %all-reduce.3.cloned.1.call-done, s32[]{:T(128)S(6)} %select_n.24, f32[2048,32]{0,1:T(8,128)S(1)} %copy-done.4), kind=kOutput, calls=%fused_computation.7 | convolution fusion | flops 805339136 | bytes 8912900 | tf_op jit(solution)/shard_map/dot_general | solution.py:75
  138.2 0.0 all-gather.2.cloned.1.call-start
  138.2 70.5 %all-reduce.5.cloned.1.call-done = f32[2048,32]{0,1:T(8,128)} async-done(((f32[2048,32]{0,1:T(8,128)}), f32[2048,32]{0,1:T(8,128)}) %all-reduce.5.cloned.1.call-update) | async-done | bytes 262160 | tf_op jit(solution)/shard_map/psum | solution.py:78
  208.8 0.2 convolution_bitcast_fusion.2
  209.0 0.2 convolution_add_fusion.1
  209.2 16.9 %all-gather.2.cloned.1.call-done = f32[8192,32]{0,1:T(8,128)} async-done(((f32[2048,32]{0,1:T(8,128)}), f32[8192,32]{0,1:T(8,128)}) %all-gather.2.cloned.1.call-update) | async-done | bytes 1048592 | tf_op jit(solution)/shard_map/all_gather | solution.py:79
  226.1 3.5 %fusion.8 = bf16[128,32]{1,0:T(8,128)(2,1)S(1)} fusion(f32[8192,32]{0,1:T(8,128)} %all-gather.2.cloned.1.call-done, s32[128]{0:T(128)S(1)} %bitcast.46, pred[128]{0:T(512)(128)(4,1)S(1)} %iota_compare_fusion.3), kind=kOutput, calls=%fused_computation.11 | convolution fusion | flops 404754432 | bytes 1057408 | tf_op jit(solution)/shard_map/dot_general | solution.py:82
  229.6 0.8 fusion.13
  230.4 0.7 copy.21
  (24 shorter events, 0.3 us)
Async XLA Ops:
  7.2 1.0 copy-start
  7.2 63.8 %reduce-scatter.2.cloned.1.call-start = ((), (), s32[]{:S(2)}) async-start(), calls=%async_computation.1 | async-start | bytes 1310720 | tf_op jit(solution)/shard_map/reduce_scatter | solution.py:61
  9.1 29.1 %copy-start.7 = (s32[1,1,1,128]{3,2,1,0:T(1,128)S(1)}, s32[1,1,1,128]{3,2,1,0:T(1,128)}, u32[]{:S(2)}) copy-start(s32[1,1,1,128]{3,2,1,0:T(1,128)} %param.18) | copy-start | bytes 1540
  9.1 117.4 %copy-start.4 = (f32[2048,32]{0,1:T(8,128)S(1)}, f32[2048,32]{0,1:T(8,128)}, u32[]{:S(2)}) copy-start(f32[2048,32]{0,1:T(8,128)} %param.20) | copy-start | bytes 786436
  9.1 7.1 %collective-permute-start = (f32[640,32]{0,1:T(8,128)S(1)}, f32[640,32]{0,1:T(8,128)S(1)}, u32[]{:S(2)}, u32[]{:S(2)}) collective-permute-start(f32[640,32]{0,1:T(8,128)S(1)} %get-tuple-element.145), channel_id=1, source_target_pairs={{0,8},{8,16},{16,24},{1,9},{9,17},{17,25},{2,10},{10,18},{18,26},{... | collective-permute-start | bytes 245768 | tf_op jit(solution)/shard_map/while/body/eval_jaxpr/ppermute | solution.py:10
  19.4 6.3 %collective-permute-start = (f32[640,32]{0,1:T(8,128)S(1)}, f32[640,32]{0,1:T(8,128)S(1)}, u32[]{:S(2)}, u32[]{:S(2)}) collective-permute-start(f32[640,32]{0,1:T(8,128)S(1)} %get-tuple-element.145), channel_id=1, source_target_pairs={{0,8},{8,16},{16,24},{1,9},{9,17},{17,25},{2,10},{10,18},{18,26},{... | collective-permute-start | bytes 245768 | tf_op jit(solution)/shard_map/while/body/eval_jaxpr/ppermute | solution.py:10
  28.8 6.3 %collective-permute-start = (f32[640,32]{0,1:T(8,128)S(1)}, f32[640,32]{0,1:T(8,128)S(1)}, u32[]{:S(2)}, u32[]{:S(2)}) collective-permute-start(f32[640,32]{0,1:T(8,128)S(1)} %get-tuple-element.145), channel_id=1, source_target_pairs={{0,8},{8,16},{16,24},{1,9},{9,17},{17,25},{2,10},{10,18},{18,26},{... | collective-permute-start | bytes 245768 | tf_op jit(solution)/shard_map/while/body/eval_jaxpr/ppermute | solution.py:10
  41.5 84.9 %all-reduce.3.cloned.1.call-start = ((), (), s32[]{:S(2)}) async-start(), calls=%async_computation.2 | async-start | bytes 524288 | tf_op jit(solution)/shard_map/psum | solution.py:69
  71.0 137.7 %all-reduce.5.cloned.1.call-start = ((), (), s32[]{:S(2)}) async-start(), calls=%async_computation.3 | async-start | bytes 524288 | tf_op jit(solution)/shard_map/psum | solution.py:78
  71.1 137.7 %copy-start.2 = (bf16[1,1,1,1,256,640]{5,4,3,2,1,0:T(8,128)(2,1)S(1)}, bf16[1,1,1,1,256,640]{5,4,3,2,1,0:T(8,128)(2,1)}, u32[]{:S(2)}) copy-start(bf16[1,1,1,1,256,640]{5,4,3,2,1,0:T(8,128)(2,1)} %param.16) | copy-start | bytes 983044
  71.1 137.9 %copy-start.3 = (bf16[1,1,1,1,256,256]{5,4,3,2,1,0:T(8,128)(2,1)S(1)}, bf16[1,1,1,1,256,256]{5,4,3,2,1,0:T(8,128)(2,1)}, u32[]{:S(2)}) copy-start(bf16[1,1,1,1,256,256]{5,4,3,2,1,0:T(8,128)(2,1)} %param.15) | copy-start | bytes 393220
  71.1 137.9 %copy-start.6 = (bf16[1,1,1,1,256,32]{4,5,3,2,1,0:T(8,128)(2,1)S(1)}, bf16[1,1,1,1,256,32]{4,5,3,2,1,0:T(8,128)(2,1)}, u32[]{:S(2)}) copy-start(bf16[1,1,1,1,256,32]{4,5,3,2,1,0:T(8,128)(2,1)} %param.12) | copy-start | bytes 49156
  138.2 91.4 %copy-start.5 = (bf16[1,1,1,1,256,128]{5,4,3,2,1,0:T(8,128)(2,1)S(1)}, bf16[1,1,1,1,256,128]{5,4,3,2,1,0:T(8,128)(2,1)}, u32[]{:S(2)}) copy-start(bf16[1,1,1,1,256,128]{5,4,3,2,1,0:T(8,128)(2,1)} %param.17) | copy-start | bytes 196612
  138.2 87.9 %all-gather.2.cloned.1.call-start = ((), (), s32[]{:S(2)}) async-start(), calls=%async_computation.4 | async-start | bytes 1310720 | tf_op jit(solution)/shard_map/all_gather | solution.py:79
  208.7 21.6 %copy-start.1 = (f32[2048,32]{0,1:T(8,128)S(1)}, f32[2048,32]{0,1:T(8,128)}, u32[]{:S(2)}) copy-start(f32[2048,32]{0,1:T(8,128)} %all-reduce.5.cloned.1.call-done) | copy-start | bytes 786436
Sparse Core Ops, SparseCore 0:
  41.6 29.3 reduce-scatter.1
  74.1 52.3 all-reduce.2
  138.3 70.3 all-reduce.4
  210.2 15.8 all-gather.1
where the time goes:
time: 238 us
  waiting for transfers between devices  178 us (75%)
  matrix products  29.7 us (12%)
  between operations  14.6 us (6%)
  starting transfers between devices  13.8 us (6%)
    psum x1, waiting for transfers between devices, body(): owned_rows = lax.psum(partial_value, ('leaf', 'row'))  70.5 us
    psum x1, waiting for transfers between devices, body(): top_block = lax.psum(top_block, ('row', 'top'))  55.4 us
    reduce_scatter x1, waiting for transfers between devices, body(): lax.psum_scatter(jnp.dot(match_table, chosen_entries, precision=largest_l...  29.4 us
    all_gather x1, waiting for transfers between devices, body(): shard_piece = lax.all_gather(owned_rows, 'top', axis=0, tiled=True)  16.9 us
    ppermute x3, starting transfers between devices, passed_along(): lax.ppermute(value, axis, [(source, source + steps) for source in range(f...  13.7 us
    dot_general x1, matrix products, body(): jnp.dot(top_inverse, rhs_piece, precision=largest_level, preferred_elemen...  11.7 us
    dot_general x3, matrix products, advance(): jnp.dot(combine_operator, earlier, precision=largest_level, preferred_ele...  9.17 us
    ppermute x3, waiting for transfers between devices, passed_along(): lax.ppermute(value, axis, [(source, source + steps) for source in range(f...  6.09 us
  transfers between devices with their start and end apart: 7, of which 7 were waited for; matrix products, arithmetic and copies ran while one was open for 0% of the time, Pallas kernels for 0%

commit v1 on v0

--- a/solution.py
+++ b/solution.py
@@ -1,7 +1,509 @@
+import functools
+
 import jax
 import jax.numpy as jnp
 from jax import lax
+from jax.experimental import pallas as pl
+from jax.experimental.pallas import tpu as pltpu
 from jax.sharding import PartitionSpec as P
+
+LANES = 128
+MESH = pl.DeviceIdType.MESH
+
+
+def nt(a, b):
+    return lax.dot_general(a, b, (((1,), (1,)), ((), ())), preferred_element_type=jnp.float32)
+
+
+def split(value):
+    high = value.astype(jnp.bfloat16)
+    low = (value - high.astype(jnp.float32)).astype(jnp.bfloat16)
+    return high, low
+
+
+def fold(value):
+    half = value.shape[0] // 2
+    return value[:half] + value[half:]
+
+
+def fused_kernel(
+    sizes,
+    loads_ref,
+    ids_ref,
+    top_loads_ref,
+    flux_hbm,
+    chain_hbm,
+    leaf_hbm,
+    edge_hbm,
+    top_hbm,
+    inverse_hbm,
+    solution_ref,
+    values_ref,
+    flux_maps,
+    chain,
+    leaf_maps,
+    edge_maps,
+    top_maps,
+    inverse,
+    chain_high,
+    chain_low,
+    inverse_high,
+    inverse_low,
+    fluxes,
+    state,
+    carry,
+    early,
+    ids,
+    entries,
+    scatter_table,
+    gather_table,
+    rhs,
+    partials,
+    arrived,
+    values,
+    picked,
+    boundary,
+    load_sem,
+    carry_sem,
+    id_leaf_send,
+    id_leaf_recv,
+    id_cell_send,
+    id_cell_recv,
+    entry_leaf_send,
+    entry_leaf_recv,
+    entry_cell_send,
+    entry_cell_recv,
+    part_send,
+    part_recv,
+    value_send,
+    value_recv,
+    bound_send,
+    bound_recv,
+):
+    L, R, T = sizes
+    cells, owners = R * T, L * R
+    leaf, row, top = lax.axis_index("leaf"), lax.axis_index("row"), lax.axis_index("top")
+    cell = row * T + top
+    owner = leaf * R + row
+    nrhs = loads_ref.shape[0]
+    slots = ids_ref.shape[1]
+    chunk = inverse.shape[0] // owners
+    columns = inverse.shape[1]
+    block_rows = inverse.shape[0]
+
+    def along(start, size):
+        return pl.ds(pl.multiple_of(start * size, size), size)
+
+    def send(src, dst, send_sem, recv_sem, where):
+        return pltpu.make_async_remote_copy(
+            src_ref=src,
+            dst_ref=dst,
+            send_sem=send_sem,
+            recv_sem=recv_sem,
+            device_id=where,
+            device_id_type=MESH,
+        )
+
+    def cell_of(step):
+        other = lax.rem(cell + step, cells)
+        return other, {"row": other // T, "top": lax.rem(other, T)}
+
+    def owner_of(step):
+        other = lax.rem(owner + step, owners)
+        return other, {"leaf": other // R, "row": lax.rem(other, R)}
+
+    def leaf_of(step):
+        other = lax.rem(leaf + step, L)
+        return other, {"leaf": other}
+
+    def top_of(step):
+        other = lax.rem(top + step, T)
+        return other, {"top": other}
+
+    pairs = (
+        (flux_hbm, flux_maps),
+        (chain_hbm, chain),
+        (inverse_hbm, inverse),
+        (leaf_hbm, leaf_maps),
+        (edge_hbm, edge_maps),
+        (top_hbm, top_maps),
+    )
+    fetches = [
+        pltpu.make_async_copy(src, dst, load_sem.at[i]) for i, (src, dst) in enumerate(pairs)
+    ]
+    for fetch in fetches:
+        fetch.start()
+
+    barrier = pltpu.get_barrier_semaphore()
+    for step in range(1, cells):
+        pl.semaphore_signal(barrier, inc=1, device_id=cell_of(step)[1], device_id_type=MESH)
+    for step in range(1, owners):
+        pl.semaphore_signal(barrier, inc=1, device_id=owner_of(step)[1], device_id_type=MESH)
+    pl.semaphore_wait(barrier, cells + owners - 2)
+
+    mine = cell * L + leaf
+    id_copies = [
+        send(
+            ids_ref,
+            ids.at[:, along(mine, slots)],
+            id_leaf_send.at[step - 1],
+            id_leaf_recv.at[step - 1],
+            leaf_of(step)[1],
+        )
+        for step in range(1, L)
+    ]
+    for copy in id_copies:
+        copy.start()
+    ids[:, along(mine, slots)] = ids_ref[...]
+
+    fetches[0].wait()
+    fluxes[...] = nt(loads_ref[...], flux_maps[...])
+    state[...] = fluxes[...]
+
+    for copy in id_copies:
+        copy.wait()
+    id_cells = [
+        send(
+            ids.at[:, along(cell, L * slots)],
+            ids.at[:, along(cell, L * slots)],
+            id_cell_send.at[step - 1],
+            id_cell_recv.at[step - 1],
+            cell_of(step)[1],
+        )
+        for step in range(1, cells)
+    ]
+    for copy in id_cells:
+        copy.start()
+
+    fetches[1].wait()
+
+    @pl.when(leaf > 0)
+    def _():
+        high, low = split(chain[...])
+        chain_high[...] = high
+        chain_low[...] = low
+
+    for copy in id_cells:
+        copy.wait()
+
+    def prepare():
+        @pl.loop(0, columns // 32)
+        def _(i):
+            start = pl.multiple_of(i * 32, 32)
+            numbers = lax.broadcasted_iota(jnp.int32, (32, ids.shape[1]), 0)
+            hit = (numbers + (owner * columns + start)) == ids[0:1, :]
+            scatter_table[pl.ds(start, 32), :] = jnp.where(hit, 1.0, 0.0).astype(jnp.bfloat16)
+
+        @pl.loop(0, block_rows // 64)
+        def _(i):
+            start = pl.multiple_of(i * 64, 64)
+            numbers = lax.broadcasted_iota(jnp.int32, (64, slots), 0) + (top * block_rows + start)
+            for other in range(T):
+                wanted = ids[0:1, along((row * T + other) * L + leaf, slots)]
+                gather_table[pl.ds(start, 64), other * slots : (other + 1) * slots] = jnp.where(
+                    numbers == wanted, 1.0, 0.0
+                ).astype(jnp.bfloat16)
+
+        fetches[2].wait()
+
+        @pl.loop(0, block_rows // 64)
+        def _(i):
+            start = pl.multiple_of(i * 64, 64)
+            high, low = split(inverse[pl.ds(start, 64), :])
+            inverse_high[pl.ds(start, 64), :] = high
+            inverse_low[pl.ds(start, 64), :] = low
+
+    def entry_leaf(step):
+        return send(
+            state.at[:, pl.ds(0, slots)],
+            entries.at[:, along(mine, slots)],
+            entry_leaf_send.at[step - 1],
+            entry_leaf_recv.at[leaf],
+            leaf_of(step)[1],
+        )
+
+    def entry_landed(source):
+        return pltpu.make_async_copy(
+            entries.at[:, along(cell * L + source, slots)],
+            entries.at[:, along(cell * L + source, slots)],
+            entry_leaf_recv.at[source],
+        )
+
+    def entry_cell(source, step):
+        number = cell * L + source
+        return send(
+            entries.at[:, along(number, slots)],
+            entries.at[:, along(number, slots)],
+            entry_cell_send.at[source * cells + step],
+            entry_cell_recv.at[number],
+            cell_of(step)[1],
+        )
+
+    next_carry = send(state, carry, carry_sem.at[0], carry_sem.at[1], leaf_of(1)[1])
+
+    def forward(source):
+        @pl.when(leaf != source)
+        def _():
+            entry_landed(source).wait()
+
+        for step in range(1, cells):
+            entry_cell(source, step).start()
+
+    @pl.loop(0, L)
+    def _(k):
+        @pl.when(leaf == k)
+        def _():
+            @pl.when(k > 0)
+            def _():
+                next_carry.wait_recv()
+                high, low = split(carry[...])
+                both = jnp.concatenate([high, low], axis=0)
+                state[...] = (
+                    fluxes[...] + fold(nt(both, chain_high[...])) + nt(high, chain_low[...])
+                )
+
+            @pl.when(k < L - 1)
+            def _():
+                next_carry.start()
+
+            for step in range(1, L):
+                entry_leaf(step).start()
+            entries[:, along(mine, slots)] = state[:, :slots]
+
+        @pl.when(k > 0)
+        def _():
+            forward(k - 1)
+
+        @pl.when(lax.rem(leaf + L // 2, L) == k)
+        def _():
+            prepare()
+
+    forward(L - 1)
+
+    fetches[3].wait()
+    fetches[4].wait()
+    fetches[5].wait()
+    early[...] = nt(loads_ref[...], leaf_maps[...]) + nt(
+        state[...].astype(jnp.bfloat16), edge_maps[...]
+    )
+
+    @pl.when(leaf < L - 1)
+    def _():
+        next_carry.wait_send()
+
+    for step in range(1, L):
+        entry_leaf(step).wait_send()
+
+    for step in range(1, cells):
+        other, _ = cell_of(step)
+        for source in range(L):
+            number = other * L + source
+            pltpu.make_async_copy(
+                entries.at[:, along(number, slots)],
+                entries.at[:, along(number, slots)],
+                entry_cell_recv.at[number],
+            ).wait()
+
+    high, low = split(entries[...])
+    both = jnp.concatenate([high, low], axis=0)
+    width = 256
+
+    @pl.loop(0, columns // width)
+    def _(i):
+        start = pl.multiple_of(i * width, width)
+        total = fold(nt(both, scatter_table[pl.ds(start, width), :]))
+        here = top_loads_ref[:, pl.ds(pl.multiple_of(row * columns + start, width), width)]
+        high, low = split(here - total)
+        rhs[0:nrhs, pl.ds(start, width)] = high
+        rhs[nrhs : 2 * nrhs, pl.ds(start, width)] = low
+
+    def product(number):
+        rows = along(number, chunk)
+        return fold(nt(rhs[...], inverse_high[rows, :])) + nt(rhs[0:nrhs, :], inverse_low[rows, :])
+
+    def part_copy(step):
+        where = owner_of(step)[1]
+        return send(
+            partials.at[step],
+            arrived.at[step],
+            part_send.at[step],
+            part_recv.at[step],
+            where,
+        )
+
+    @pl.loop(1, owners)
+    def _(step):
+        partials[step] = product(owner_of(step)[0])
+        part_copy(step).start()
+
+    total = product(owner)
+    for step in range(1, owners):
+        part_copy(step).wait_recv()
+        total = total + arrived[step]
+    values[:, along(owner, chunk)] = total
+
+    def value_copy(step):
+        where = owner_of(step)[1]
+        return send(
+            values.at[:, along(owner, chunk)],
+            values.at[:, along(owner, chunk)],
+            value_send.at[step],
+            value_recv.at[step],
+            where,
+        )
+
+    for step in range(1, owners):
+        value_copy(step).start()
+    for step in range(1, owners):
+        part_copy(step).wait_send()
+    for step in range(1, owners):
+        value_copy(step).wait_recv()
+
+    final = values[...]
+    values_ref[...] = final
+    gathered = jnp.dot(
+        final.astype(jnp.bfloat16), gather_table[...], preferred_element_type=jnp.float32
+    )
+    for other in range(T):
+        picked[other] = gathered[:, other * slots : (other + 1) * slots]
+
+    def bound_copy(step):
+        other, where = top_of(step)
+        return send(
+            picked.at[other], boundary.at[step], bound_send.at[step], bound_recv.at[step], where
+        )
+
+    for step in range(1, T):
+        bound_copy(step).start()
+    bound = picked[top]
+    for step in range(1, T):
+        bound_copy(step).wait_recv()
+        bound = bound + boundary[step]
+    late = nt(bound.astype(jnp.bfloat16), top_maps[...])
+    solution_ref[...] = (early[...] + late).astype(jnp.bfloat16)
+
+    for source in range(L):
+        for step in range(1, cells):
+            entry_cell(source, step).wait_send()
+    for step in range(1, owners):
+        value_copy(step).wait_send()
+    for step in range(1, T):
+        bound_copy(step).wait_send()
+
+
+def fused_body(
+    sizes,
+    loads,
+    flux_maps,
+    chain_maps,
+    leaf_maps,
+    edge_maps,
+    top_maps,
+    slot_nodes,
+    slot_counts,
+    top_loads,
+    top_inverse,
+):
+    L, R, T = sizes
+    cells, owners = R * T, L * R
+    node_count, nrhs = loads.shape[4:]
+    sep_width = chain_maps.shape[-1]
+    slots = slot_nodes.shape[-1]
+    block_rows, columns = top_inverse.shape
+    chunk = block_rows // owners
+    everyone = L * cells
+    f32, bf16 = jnp.float32, jnp.bfloat16
+    nodes = slot_nodes.reshape(1, slots)
+    live = lax.broadcasted_iota(jnp.int32, (8, slots), 1) < slot_counts.reshape(1, 1)
+    ids = jnp.where(live, nodes, -1)
+    dma = pltpu.SemaphoreType.DMA
+    vmem = pl.BlockSpec(memory_space=pltpu.VMEM)
+    anywhere = pl.BlockSpec(memory_space=pl.ANY)
+    solution, values = pl.pallas_call(
+        functools.partial(fused_kernel, sizes),
+        out_shape=(
+            jax.ShapeDtypeStruct((nrhs, node_count), bf16),
+            jax.ShapeDtypeStruct((nrhs, block_rows), f32),
+        ),
+        in_specs=[vmem] * 3 + [anywhere] * 6,
+        out_specs=(vmem, vmem),
+        scratch_shapes=[
+            pltpu.VMEM((sep_width, node_count), bf16),
+            pltpu.VMEM((sep_width, sep_width), f32),
+            pltpu.VMEM((node_count, node_count), bf16),
+            pltpu.VMEM((node_count, sep_width), bf16),
+            pltpu.VMEM((node_count, slots), bf16),
+            pltpu.VMEM((block_rows, columns), f32),
+            pltpu.VMEM((sep_width, sep_width), bf16),
+            pltpu.VMEM((sep_width, sep_width), bf16),
+            pltpu.VMEM((block_rows, columns), bf16),
+            pltpu.VMEM((block_rows, columns), bf16),
+            pltpu.VMEM((nrhs, sep_width), f32),
+            pltpu.VMEM((nrhs, sep_width), f32),
+            pltpu.VMEM((nrhs, sep_width), f32),
+            pltpu.VMEM((nrhs, node_count), f32),
+            pltpu.VMEM((8, everyone * slots), jnp.int32),
+            pltpu.VMEM((nrhs, everyone * slots), f32),
+            pltpu.VMEM((columns, everyone * slots), bf16),
+            pltpu.VMEM((block_rows, T * slots), bf16),
+            pltpu.VMEM((2 * nrhs, columns), bf16),
+            pltpu.VMEM((owners, nrhs, chunk), f32),
+            pltpu.VMEM((owners, nrhs, chunk), f32),
+            pltpu.VMEM((nrhs, block_rows), f32),
+            pltpu.VMEM((T, nrhs, slots), f32),
+            pltpu.VMEM((T, nrhs, slots), f32),
+            dma((6,)),
+            dma((2,)),
+            dma((L,)),
+            dma((L,)),
+            dma((cells,)),
+            dma((cells,)),
+            dma((L,)),
+            dma((L,)),
+            dma((everyone,)),
+            dma((everyone,)),
+            dma((owners,)),
+            dma((owners,)),
+            dma((owners,)),
+            dma((owners,)),
+            dma((T,)),
+            dma((T,)),
+        ],
+        compiler_params=pltpu.CompilerParams(
+            collective_id=0, has_side_effects=True, vmem_limit_bytes=56 << 20
+        ),
+    )(
+        loads.reshape(node_count, nrhs).T,
+        ids,
+        top_loads.T,
+        flux_maps.reshape(sep_width, node_count),
+        chain_maps.reshape(sep_width, sep_width),
+        leaf_maps.reshape(node_count, node_count),
+        edge_maps.reshape(node_count, sep_width),
+        top_maps.reshape(node_count, slots),
+        top_inverse,
+    )
+    return solution.T.reshape(1, 1, 1, 1, node_count, nrhs), values.T
+
+
+def fits(sizes, loads, chain_maps, slot_nodes, top_loads, top_inverse):
+    L, R, T = sizes
+    owners = L * R
+    block_rows, columns = top_inverse.shape
+    slots = slot_nodes.shape[-1]
+    everyone = owners * T * slots
+    return (
+        min(sizes) > 1
+        and loads.shape[3] == 1
+        and loads.shape[5] % 16 == 0
+        and slots == LANES
+        and chain_maps.shape[-1] % LANES == 0
+        and loads.shape[4] % LANES == 0
+        and columns % 256 == 0
+        and block_rows % (owners * LANES) == 0
+        and top_loads.shape[0] == R * columns
+        and columns * everyone * 2 + block_rows * columns * 8 < (32 << 20)
+    )
 
 
 def passed_along(value, axis, steps):
@@ -10,7 +512,7 @@
     return lax.ppermute(value, axis, [(source, source + steps) for source in range(first, last)])
 
 
-def body(
+def plain_body(
     loads,
     flux_maps,
     chain_maps,
@@ -106,7 +608,15 @@
     return (solution, owned_rows)
 
 
+def body(sizes, *arrays):
+    loads, _, chain_maps, _, _, _, slot_nodes, _, top_loads, top_inverse = arrays
+    if fits(sizes, loads, chain_maps, slot_nodes, top_loads, top_inverse):
+        return fused_body(sizes, *arrays)
+    return plain_body(*arrays)
+
+
 def solution(mesh):
+    sizes = tuple(mesh.shape[axis] for axis in ("leaf", "row", "top"))
     in_specs = (
         P("leaf", "row", "top", None, None, None),
         P("leaf", "row", "top", None, None),
@@ -120,4 +630,10 @@
         P("top", ("leaf", "row")),
     )
     out_specs = (P("leaf", "row", "top", None, None, None), P("top", None))
-    return jax.shard_map(body, mesh=mesh, in_specs=in_specs, out_specs=out_specs, check_vma=False)
+    return jax.shard_map(
+        functools.partial(body, sizes),
+        mesh=mesh,
+        in_specs=in_specs,
+        out_specs=out_specs,
+        check_vma=False,
+    )

time: 238 us -> 62.2 us (0.26)
  waiting for transfers between devices: 178 us -> 0 us
  Pallas kernels: 0 us -> 56.4 us
  matrix products: 29.7 us -> 0 us
  starting transfers between devices: 13.8 us -> 0 us
  between operations: 14.6 us -> 1.29 us
    psum x2 -> x0, waiting for transfers between devices: 126 us -> none  [the longest x1 70.5 us: body(): owned_rows = lax.psum(partial_value, ('leaf', 'row'))]
    pallas_call x0 -> x1, Pallas kernels: none -> 56.4 us  [fused_body(): pl.pallas_call(functools.partial(fused_kernel, sizes), out_shape=(jax.Sha...]
    dot_general x10 -> x0, matrix products: 29.7 us -> none  [the longest x1 11.7 us: body(): jnp.dot(top_inverse, rhs_piece, precision=largest_level, preferred_elemen...]
    reduce_scatter x1 -> x0, waiting for transfers between devices: 29.4 us -> none  [body(): lax.psum_scatter(jnp.dot(match_table, chosen_entries, precision=largest_l...]
    all_gather x1 -> x0, waiting for transfers between devices: 16.9 us -> none  [body(): shard_piece = lax.all_gather(owned_rows, 'top', axis=0, tiled=True)]
    ppermute x3 -> x0, starting transfers between devices: 13.7 us -> none  [passed_along(): lax.ppermute(value, axis, [(source, source + steps) for source in range(f...]
    ppermute x3 -> x0, waiting for transfers between devices: 6.09 us -> none  [passed_along(): lax.ppermute(value, axis, [(source, source + steps) for source in range(f...]
  transfers between devices with their start and end apart: 7 -> 0, of which waited for: 7 -> 0; matrix products, arithmetic and copies ran while one was open for 0% -> 0% of each run, Pallas kernels for 0% -> 0%
where the time goes in v1:
time: 62.2 us; the launch traced here: 61.9 us
  Pallas kernels  56.4 us (91%)
  local copies, waits for them, and re-layouts  2.99 us (5%)
  between operations  1.29 us (2%)
  other arithmetic  1.26 us (2%)
    pallas_call x1, Pallas kernels, fused_body(): pl.pallas_call(functools.partial(fused_kernel, sizes), out_shape=(jax.Sha...  56.4 us
    unnamed x2, local copies, waits for them, and re-layouts  2.99 us
    select_n x1, other arithmetic, fused_body(): ids = jnp.where(live, nodes, -1)  1.25 us

profile of v1, /device:TPU:0, one launch (start us, length us, event | category | flops | bytes accessed | tf_op | source)
XLA Modules:
  0.0 61.9 jit_solution(365489407730012951)
XLA Ops:
  1.3 1.3 %broadcast_select_fusion.ids_ref = s32[8,128]{1,0:T(8,128)} fusion(s32[128]{0:T(128)} %bitcast.25, pred[128]{0:T(512)(128)(4,1)S(1)} %iota_compare_fusion), kind=kLoop, calls=%fused_computation | loop fusion | flops 1024 | bytes 4736 | tf_op jit(solution)/shard_map/jit(_where)/select_n | solution.py:418
  2.5 56.4 %shard_map.113 = (bf16[32,256]{1,0:T(8,128)(2,1)}, f32[32,2048]{1,0:T(8,128)}) custom-call(bf16[32,256]{1,0:T(8,128)(2,1)} %bitcast.23, s32[8,128]{1,0:T(8,128)} %broadcast_select_fusion.ids_ref, f32[32,2048]{1,0:T(8,128)} %bitcast.19, bf16[640,256]{1,0:T(8,128)(2,1)} %bitcast.17, f32[640,640]{1,0:T(8,128)} %bitcast.16, bf16[256,256]{1,0:T(8,128)(2,1)} %bitcast.21, ...), custom_call_target="tpu_custom_call" | custom-call | tf_op jit(solution)/shard_map/pallas_call | solution.py:422
  58.9 1.3 %copy.15 = bf16[1,1,1,1,256,32]{4,5,3,2,1,0:T(8,128)(2,1)} copy(bf16[1,1,1,1,256,32]{4,5,3,2,1,0:T(8,128)(2,1)} %bitcast.24) | data formatting | bytes 32768
  60.3 1.7 %copy.16 = f32[2048,32]{0,1:T(8,128)} copy(f32[2048,32]{0,1:T(8,128)} %bitcast.20) | data formatting | bytes 524288
  (1 shorter events, 0.0 us)

commit v2 on v1

--- a/solution.py
+++ b/solution.py
@@ -29,8 +29,9 @@
 def fused_kernel(
     sizes,
     loads_ref,
-    ids_ref,
-    top_loads_ref,
+    nodes_ref,
+    count_ref,
+    top_loads_hbm,
     flux_hbm,
     chain_hbm,
     leaf_hbm,
@@ -38,7 +39,9 @@
     top_hbm,
     inverse_hbm,
     solution_ref,
-    values_ref,
+    values_hbm,
+    top_loads,
+    own_ids,
     flux_maps,
     chain,
     leaf_maps,
@@ -64,7 +67,8 @@
     picked,
     boundary,
     load_sem,
-    carry_sem,
+    carry_send,
+    carry_recv,
     id_leaf_send,
     id_leaf_recv,
     id_cell_send,
@@ -86,7 +90,7 @@
     cell = row * T + top
     owner = leaf * R + row
     nrhs = loads_ref.shape[0]
-    slots = ids_ref.shape[1]
+    slots = nodes_ref.shape[1]
     chunk = inverse.shape[0] // owners
     columns = inverse.shape[1]
     block_rows = inverse.shape[0]
@@ -127,6 +131,7 @@
         (leaf_hbm, leaf_maps),
         (edge_hbm, edge_maps),
         (top_hbm, top_maps),
+        (top_loads_hbm.at[:, along(row, columns)], top_loads),
     )
     fetches = [
         pltpu.make_async_copy(src, dst, load_sem.at[i]) for i, (src, dst) in enumerate(pairs)
@@ -139,12 +144,27 @@
         pl.semaphore_signal(barrier, inc=1, device_id=cell_of(step)[1], device_id_type=MESH)
     for step in range(1, owners):
         pl.semaphore_signal(barrier, inc=1, device_id=owner_of(step)[1], device_id_type=MESH)
+    live = lax.broadcasted_iota(jnp.int32, own_ids.shape, 1) < count_ref[...]
+    own_ids[...] = jnp.where(live, nodes_ref[...], -1)
+    mine = cell * L + leaf
+    ids[:, along(mine, slots)] = own_ids[...]
+
+    fetches[0].wait()
+    fluxes[...] = nt(loads_ref[...], flux_maps[...])
+    state[...] = fluxes[...]
+    fetches[1].wait()
+
+    @pl.when(leaf > 0)
+    def _():
+        high, low = split(chain[...])
+        chain_high[...] = high
+        chain_low[...] = low
+
     pl.semaphore_wait(barrier, cells + owners - 2)
 
-    mine = cell * L + leaf
     id_copies = [
         send(
-            ids_ref,
+            own_ids,
             ids.at[:, along(mine, slots)],
             id_leaf_send.at[step - 1],
             id_leaf_recv.at[step - 1],
@@ -152,16 +172,6 @@
         )
         for step in range(1, L)
     ]
-    for copy in id_copies:
-        copy.start()
-    ids[:, along(mine, slots)] = ids_ref[...]
-
-    fetches[0].wait()
-    fluxes[...] = nt(loads_ref[...], flux_maps[...])
-    state[...] = fluxes[...]
-
-    for copy in id_copies:
-        copy.wait()
     id_cells = [
         send(
             ids.at[:, along(cell, L * slots)],
@@ -172,27 +182,24 @@
         )
         for step in range(1, cells)
     ]
-    for copy in id_cells:
-        copy.start()
-
-    fetches[1].wait()
-
-    @pl.when(leaf > 0)
-    def _():
-        high, low = split(chain[...])
-        chain_high[...] = high
-        chain_low[...] = low
-
-    for copy in id_cells:
-        copy.wait()
-
-    def prepare():
+
+    def prepare_tables():
+        for copy in id_cells:
+            copy.wait()
+
         @pl.loop(0, columns // 32)
         def _(i):
             start = pl.multiple_of(i * 32, 32)
-            numbers = lax.broadcasted_iota(jnp.int32, (32, ids.shape[1]), 0)
-            hit = (numbers + (owner * columns + start)) == ids[0:1, :]
-            scatter_table[pl.ds(start, 32), :] = jnp.where(hit, 1.0, 0.0).astype(jnp.bfloat16)
+            numbers = lax.broadcasted_iota(jnp.int32, (32, slots), 0) + (owner * columns + start)
+            for source in range(L):
+                for other in range(cells):
+                    wanted = other * L + source
+                    place = source * cells + other
+                    scatter_table[pl.ds(start, 32), place * slots : (place + 1) * slots] = (
+                        jnp.where(
+                            numbers == ids[0:1, wanted * slots : (wanted + 1) * slots], 1.0, 0.0
+                        ).astype(jnp.bfloat16)
+                    )
 
         @pl.loop(0, block_rows // 64)
         def _(i):
@@ -204,6 +211,7 @@
                     numbers == wanted, 1.0, 0.0
                 ).astype(jnp.bfloat16)
 
+    def prepare_inverse():
         fetches[2].wait()
 
         @pl.loop(0, block_rows // 64)
@@ -216,7 +224,7 @@
     def entry_leaf(step):
         return send(
             state.at[:, pl.ds(0, slots)],
-            entries.at[:, along(mine, slots)],
+            entries.at[:, along(leaf * cells + cell, slots)],
             entry_leaf_send.at[step - 1],
             entry_leaf_recv.at[leaf],
             leaf_of(step)[1],
@@ -224,13 +232,13 @@
 
     def entry_landed(source):
         return pltpu.make_async_copy(
-            entries.at[:, along(cell * L + source, slots)],
-            entries.at[:, along(cell * L + source, slots)],
+            entries.at[:, along(source * cells + cell, slots)],
+            entries.at[:, along(source * cells + cell, slots)],
             entry_leaf_recv.at[source],
         )
 
     def entry_cell(source, step):
-        number = cell * L + source
+        number = source * cells + cell
         return send(
             entries.at[:, along(number, slots)],
             entries.at[:, along(number, slots)],
@@ -239,7 +247,48 @@
             cell_of(step)[1],
         )
 
-    next_carry = send(state, carry, carry_sem.at[0], carry_sem.at[1], leaf_of(1)[1])
+    spans = [(at, min(256, fluxes.shape[1] - at)) for at in range(0, fluxes.shape[1], 256)]
+
+    def carry_copy(i):
+        part = pl.ds(*spans[i])
+        return send(
+            state.at[:, part],
+            carry.at[:, part],
+            carry_send.at[i],
+            carry_recv.at[i],
+            leaf_of(1)[1],
+        )
+
+    def hand_on(i, k):
+        @pl.when(k < L - 1)
+        def _():
+            carry_copy(i).start()
+
+        if i == 0:
+            for step in range(1, L):
+                entry_leaf(step).start()
+            entries[:, along(leaf * cells + cell, slots)] = state[:, :slots]
+
+    def advance(k):
+        total = fluxes[...]
+        for i, (at, size) in enumerate(spans):
+            carry_copy(i).wait_recv()
+            high, low = split(carry[:, at : at + size])
+            both = jnp.concatenate([high, low], axis=0)
+            if i < len(spans) - 1:
+                total = (
+                    total
+                    + fold(nt(both, chain_high[:, at : at + size]))
+                    + nt(high, chain_low[:, at : at + size])
+                )
+                continue
+            for j, (to, wide) in enumerate(spans):
+                state[:, to : to + wide] = (
+                    total[:, to : to + wide]
+                    + fold(nt(both, chain_high[to : to + wide, at : at + size]))
+                    + nt(high, chain_low[to : to + wide, at : at + size])
+                )
+                hand_on(j, k)
 
     def forward(source):
         @pl.when(leaf != source)
@@ -249,71 +298,74 @@
         for step in range(1, cells):
             entry_cell(source, step).start()
 
+    @pl.when(leaf == 0)
+    def _():
+        for j in range(len(spans)):
+            hand_on(j, 0)
+
+    for copy in id_copies:
+        copy.start()
+
     @pl.loop(0, L)
     def _(k):
-        @pl.when(leaf == k)
+        @pl.when((leaf == k) & (k > 0))
         def _():
-            @pl.when(k > 0)
-            def _():
-                next_carry.wait_recv()
-                high, low = split(carry[...])
-                both = jnp.concatenate([high, low], axis=0)
-                state[...] = (
-                    fluxes[...] + fold(nt(both, chain_high[...])) + nt(high, chain_low[...])
-                )
-
-            @pl.when(k < L - 1)
-            def _():
-                next_carry.start()
-
-            for step in range(1, L):
-                entry_leaf(step).start()
-            entries[:, along(mine, slots)] = state[:, :slots]
+            advance(k)
 
         @pl.when(k > 0)
         def _():
             forward(k - 1)
 
-        @pl.when(lax.rem(leaf + L // 2, L) == k)
+        @pl.when(k == 1)
         def _():
-            prepare()
+            for copy in id_copies:
+                copy.wait()
+            for copy in id_cells:
+                copy.start()
+
+        @pl.when(k == 1 - (2 * leaf) // L)
+        def _():
+            prepare_inverse()
+
+        @pl.when(k == L // 2)
+        def _():
+            prepare_tables()
 
     forward(L - 1)
 
-    fetches[3].wait()
-    fetches[4].wait()
-    fetches[5].wait()
-    early[...] = nt(loads_ref[...], leaf_maps[...]) + nt(
-        state[...].astype(jnp.bfloat16), edge_maps[...]
-    )
-
-    @pl.when(leaf < L - 1)
-    def _():
-        next_carry.wait_send()
-
-    for step in range(1, L):
-        entry_leaf(step).wait_send()
-
-    for step in range(1, cells):
-        other, _ = cell_of(step)
-        for source in range(L):
-            number = other * L + source
+    def gathered_from(source):
+        for step in range(1, cells):
+            number = source * cells + cell_of(step)[0]
             pltpu.make_async_copy(
                 entries.at[:, along(number, slots)],
                 entries.at[:, along(number, slots)],
                 entry_cell_recv.at[number],
             ).wait()
 
-    high, low = split(entries[...])
+    fetches[6].wait()
+    width = 256
+    last = (L - 1) * cells * slots
+    for source in range(L - 1):
+        gathered_from(source)
+    high, low = split(entries[:, :last])
     both = jnp.concatenate([high, low], axis=0)
-    width = 256
 
     @pl.loop(0, columns // width)
     def _(i):
         start = pl.multiple_of(i * width, width)
-        total = fold(nt(both, scatter_table[pl.ds(start, width), :]))
-        here = top_loads_ref[:, pl.ds(pl.multiple_of(row * columns + start, width), width)]
-        high, low = split(here - total)
+        top_loads[:, pl.ds(start, width)] = top_loads[:, pl.ds(start, width)] - fold(
+            nt(both, scatter_table[pl.ds(start, width), :last])
+        )
+
+    gathered_from(L - 1)
+    high, low = split(entries[:, last:])
+    both_last = jnp.concatenate([high, low], axis=0)
+
+    @pl.loop(0, columns // width)
+    def _(i):
+        start = pl.multiple_of(i * width, width)
+        total = fold(nt(both_last, scatter_table[pl.ds(start, width), last:]))
+        high, low = split(top_loads[:, pl.ds(start, width)] - total)
         rhs[0:nrhs, pl.ds(start, width)] = high
         rhs[nrhs : 2 * nrhs, pl.ds(start, width)] = low
 
@@ -354,13 +406,19 @@
 
     for step in range(1, owners):
         value_copy(step).start()
+    for fetch in fetches[3:6]:
+        fetch.wait()
+    early[...] = nt(loads_ref[...], leaf_maps[...]) + nt(
+        state[...].astype(jnp.bfloat16), edge_maps[...]
+    )
     for step in range(1, owners):
         part_copy(step).wait_send()
     for step in range(1, owners):
         value_copy(step).wait_recv()
 
     final = values[...]
-    values_ref[...] = final
+    write = pltpu.make_async_copy(values, values_hbm, load_sem.at[7])
+    write.start()
     gathered = jnp.dot(
         final.astype(jnp.bfloat16), gather_table[...], preferred_element_type=jnp.float32
     )
@@ -382,9 +440,17 @@
     late = nt(bound.astype(jnp.bfloat16), top_maps[...])
     solution_ref[...] = (early[...] + late).astype(jnp.bfloat16)
 
+    @pl.when(leaf < L - 1)
+    def _():
+        for i in range(len(spans)):
+            carry_copy(i).wait_send()
+
+    for step in range(1, L):
+        entry_leaf(step).wait_send()
     for source in range(L):
         for step in range(1, cells):
             entry_cell(source, step).wait_send()
+    write.wait()
     for step in range(1, owners):
         value_copy(step).wait_send()
     for step in range(1, T):
@@ -414,8 +480,6 @@
     everyone = L * cells
     f32, bf16 = jnp.float32, jnp.bfloat16
     nodes = slot_nodes.reshape(1, slots)
-    live = lax.broadcasted_iota(jnp.int32, (8, slots), 1) < slot_counts.reshape(1, 1)
-    ids = jnp.where(live, nodes, -1)
     dma = pltpu.SemaphoreType.DMA
     vmem = pl.BlockSpec(memory_space=pltpu.VMEM)
     anywhere = pl.BlockSpec(memory_space=pl.ANY)
@@ -425,9 +489,11 @@
             jax.ShapeDtypeStruct((nrhs, node_count), bf16),
             jax.ShapeDtypeStruct((nrhs, block_rows), f32),
         ),
-        in_specs=[vmem] * 3 + [anywhere] * 6,
-        out_specs=(vmem, vmem),
+        in_specs=[vmem] * 3 + [anywhere] * 7,
+        out_specs=(vmem, anywhere),
         scratch_shapes=[
+            pltpu.VMEM((nrhs, columns), f32),
+            pltpu.VMEM((8, slots), jnp.int32),
             pltpu.VMEM((sep_width, node_count), bf16),
             pltpu.VMEM((sep_width, sep_width), f32),
             pltpu.VMEM((node_count, node_count), bf16),
@@ -452,8 +518,9 @@
             pltpu.VMEM((nrhs, block_rows), f32),
             pltpu.VMEM((T, nrhs, slots), f32),
             pltpu.VMEM((T, nrhs, slots), f32),
-            dma((6,)),
-            dma((2,)),
+            dma((8,)),
+            dma((-(-sep_width // 256),)),
+            dma((-(-sep_width // 256),)),
             dma((L,)),
             dma((L,)),
             dma((cells,)),
@@ -474,7 +541,8 @@
         ),
     )(
         loads.reshape(node_count, nrhs).T,
-        ids,
+        nodes,
+        slot_counts.reshape(1, 1),
         top_loads.T,
         flux_maps.reshape(sep_width, node_count),
         chain_maps.reshape(sep_width, sep_width),

time: 62.2 us -> 52.3 us (0.84)
  Pallas kernels: 56.4 us -> 47.1 us
  other arithmetic: 1.26 us -> 0 us
    pallas_call x1, Pallas kernels: 56.4 us -> 47.1 us  [fused_body(): pl.pallas_call(functools.partial(fused_kernel, sizes), out_shape=(jax.Sha...]
    select_n x1 -> x0, other arithmetic: 1.25 us -> none  [fused_body(): ids = jnp.where(live, nodes, -1)]
where the time goes in v2:
time: 52.3 us; the launch traced here: 51.4 us
  Pallas kernels  47.1 us (90%)
  local copies, waits for them, and re-layouts  2.99 us (6%)
  between operations  1.29 us (2%)
    pallas_call x1, Pallas kernels, fused_body(): pl.pallas_call(functools.partial(fused_kernel, sizes), out_shape=(jax.Sha...  47.1 us
    unnamed x2, local copies, waits for them, and re-layouts  2.99 us

profile of v2, /device:TPU:0, one launch (start us, length us, event | category | flops | bytes accessed | tf_op | source)
XLA Modules:
  0.0 51.4 jit_solution(10356024575115632713)
XLA Ops:
  1.3 47.1 %shard_map.113 = (bf16[32,256]{1,0:T(8,128)(2,1)}, f32[32,2048]{1,0:T(8,128)}) custom-call(bf16[32,256]{1,0:T(8,128)(2,1)} %bitcast.23, s32[1,128]{1,0:T(1,128)} %bitcast.25, s32[1,1]{1,0:T(1,128)} %bitcast.15.count_ref, f32[32,2048]{1,0:T(8,128)} %bitcast.19, bf16[640,256]{1,0:T(8,128)(2,1)} %bitcast.17, f32[640,640]{1,0:T(8,128)} %bitcast.16, ...), custom_call_target="tpu_custom_call" | custom-call | tf_op jit(solution)/shard_map/pallas_call | solution.py:486
  48.4 1.3 %copy.15 = bf16[1,1,1,1,256,32]{4,5,3,2,1,0:T(8,128)(2,1)} copy(bf16[1,1,1,1,256,32]{4,5,3,2,1,0:T(8,128)(2,1)} %bitcast.24) | data formatting | bytes 32768
  49.8 1.7 %copy.16 = f32[2048,32]{0,1:T(8,128)} copy(f32[2048,32]{0,1:T(8,128)} %bitcast.20) | data formatting | bytes 524288

commit v3 on v2

--- a/solution.py
+++ b/solution.py
@@ -383,8 +383,11 @@
             where,
         )
 
-    @pl.loop(1, owners)
-    def _(step):
+    half = owners // 2
+
+    @pl.loop(0, owners - 1)
+    def _(i):
+        step = jnp.where(i < half, 2 * i + 1, 2 * (i - half) + 2)
         partials[step] = product(owner_of(step)[0])
         part_copy(step).start()
 
@@ -455,6 +458,11 @@
         value_copy(step).wait_send()
     for step in range(1, T):
         bound_copy(step).wait_send()
+
+
+def finish_kernel(solution_ref, values_ref, solution_out, values_out):
+    solution_out[...] = solution_ref[...]
+    values_out[...] = values_ref[...]
 
 
 def fused_body(
@@ -551,6 +559,15 @@
         top_maps.reshape(node_count, slots),
         top_inverse,
     )
+    solution, values = pl.pallas_call(
+        finish_kernel,
+        out_shape=(
+            jax.ShapeDtypeStruct(solution.shape, solution.dtype),
+            jax.ShapeDtypeStruct(values.shape, values.dtype),
+        ),
+        in_specs=[vmem, vmem],
+        out_specs=(vmem, vmem),
+    )(solution, values)
     return solution.T.reshape(1, 1, 1, 1, node_count, nrhs), values.T
 
 

time: 52.3 us -> 49.9 us (0.954)
  local copies, waits for them, and re-layouts: 2.99 us -> 0 us
  Pallas kernels: 47.1 us -> 48.2 us
    unnamed x2 -> x0, local copies, waits for them, and re-layouts: 2.99 us -> none
    pallas_call x0 -> x1, Pallas kernels: none -> 1.69 us  [fused_body(): pl.pallas_call(finish_kernel, out_shape=(jax.ShapeDtypeStruct(solution.sh...]
    pallas_call x1, Pallas kernels: 47.1 us -> 46.5 us  [fused_body(): pl.pallas_call(functools.partial(fused_kernel, sizes), out_shape=(jax.Sha...]
where the time goes in v3:
time: 49.9 us; the launch traced here: 49.5 us
  Pallas kernels  48.2 us (97%)
  between operations  1.29 us (3%)
    pallas_call x1, Pallas kernels, fused_body(): pl.pallas_call(functools.partial(fused_kernel, sizes), out_shape=(jax.Sha...  46.5 us
    pallas_call x1, Pallas kernels, fused_body(): pl.pallas_call(finish_kernel, out_shape=(jax.ShapeDtypeStruct(solution.sh...  1.69 us

profile of v3, /device:TPU:0, one launch (start us, length us, event | category | flops | bytes accessed | tf_op | source)
XLA Modules:
  0.0 49.5 jit_solution(13897730463797644109)
XLA Ops:
  1.3 46.5 %shard_map.113 = (bf16[32,256]{1,0:T(8,128)(2,1)}, f32[32,2048]{1,0:T(8,128)}) custom-call(bf16[32,256]{1,0:T(8,128)(2,1)} %bitcast.22, s32[1,128]{1,0:T(1,128)} %bitcast.23, s32[1,1]{1,0:T(1,128)} %bitcast.15.count_ref, f32[32,2048]{1,0:T(8,128)} %bitcast.19, bf16[640,256]{1,0:T(8,128)(2,1)} %bitcast.17, f32[640,640]{1,0:T(8,128)} %bitcast.16, ...), custom_call_target="tpu_custom_call" | custom-call | tf_op jit(solution)/shard_map/pallas_call | solution.py:494
  47.8 1.7 %shard_map.114 = (bf16[32,256]{1,0:T(8,128)(2,1)}, f32[32,2048]{1,0:T(8,128)}) custom-call(bf16[32,256]{1,0:T(8,128)(2,1)} %get-tuple-element.6.solution_ref, f32[32,2048]{1,0:T(8,128)} %get-tuple-element.7.values_ref), custom_call_target="tpu_custom_call" | custom-call | tf_op jit(solution)/shard_map/pallas_call | solution.py:562
